TPU v7x, 128 devices: a whole 4x4x4 slice. The times are simulated.
128 devices in a mesh: dp: 8 (over z_lo, y), tensor: 16 (over z_hi, x, core).
Axes of the slice: x: 4, y: 4, z: 4 (z_hi: 2, z_lo: 2; z = z_hi * 2 + z_lo), core: 2. Of those that a mesh axis runs over, the one named last changes fastest.
Arguments:
- block_input: bfloat16 [16384, 1024], P(('dp', 'tensor')), may hold values from -6 to 6
- segment_ids: int32 [16, 1024], P('dp'), may hold values from 0 to 3, never falling along the last dimension, each value on 1 to 512 neighbouring positions
- qkv_weight: bfloat16 [3, 1024, 1024], P(None, None, 'tensor'), may hold values from -1 to 1
- qv_bias: float32 [2, 1024], P(None, 'tensor'), may hold values from -3 to 3
- out_weight: bfloat16 [1024, 1024], P('tensor'), may hold values from -1.5 to 1.5
- out_bias: float32 [1024], replicated, may hold values from -3 to 3
- norm1_gain: float32 [1024], replicated, may hold values from 0.5 to 1.5
- norm1_bias: float32 [1024], replicated, may hold values from -3 to 3
- up_weight: bfloat16 [1024, 4096], P(None, 'tensor'), may hold values from -0.1875 to 0.1875
- up_bias: float32 [4096], P('tensor'), may hold values from -3 to 3
- down_weight: bfloat16 [4096, 1024], P('tensor'), may hold values from -0.09375 to 0.09375
- down_bias: float32 [1024], replicated, may hold values from -3 to 3
- norm2_gain: float32 [1024], replicated, may hold values from 0.5 to 1.5
- norm2_bias: float32 [1024], replicated, may hold values from -3 to 3
- cotangent: bfloat16 [16384, 1024], P(('dp', 'tensor')), may hold values from -6 to 6
Outputs:
- layer_output: bfloat16 [16384, 1024], P(('dp', 'tensor'))
- input_grad: bfloat16 [16384, 1024], P(('dp', 'tensor'))
- grad_qkv: float32 [3, 1024, 1024], P(None, None, 'tensor')
- grad_qv_bias: float32 [2, 1024], P(None, 'tensor')
- grad_out_proj: float32 [1024, 1024], P('tensor')
- grad_out_bias: float32 [1024], replicated
- grad_gain_one: float32 [1024], replicated
- grad_bias_one: float32 [1024], replicated
- grad_up: float32 [1024, 4096], P(None, 'tensor')
- grad_up_bias: float32 [4096], P('tensor')
- grad_down: float32 [4096, 1024], P('tensor')
- grad_down_bias: float32 [1024], replicated
- grad_gain_two: float32 [1024], replicated
- grad_bias_two: float32 [1024], replicated
Inputs may be any that keep to these rules, and one draw needn't show every extreme that they name: `segment_ids`: document numbers never fall along a sequence; each document holds 1 to 512 tokens.
All inputs are finite; a program needn't handle non-finite values.
Results may differ from a plain program's by a relative error of at most 0.023.
The roundings to bfloat16 on the way count: a program that leaves them out, or rounds other values in their place, can miss the bound.
Values may be sent and summed in bfloat16 or wider, within the bound.
A program may use at most 128 MiB of HBM per device.

v0:
```python
import jax
import jax.numpy as jnp
from jax import lax
from jax.sharding import PartitionSpec as P

HEAD_DIM = 64


EPS = 1e-12
MASKED = -1e30
ROOT_HALF = 0.7071067811865476
INV_ROOT_TAU = 0.3989422804014327


def layer_norm(rows, gain, shift):
    center = rows - jnp.mean(rows, axis=-1, keepdims=True)
    inverse = lax.rsqrt(jnp.mean(center * center, axis=-1, keepdims=True) + EPS)
    normed = center * inverse
    return (normed * gain + shift, normed, inverse)


def norm_back(grad, normed, inverse, gain):
    scaled = grad * gain
    return inverse * (
        scaled
        - jnp.mean(scaled, axis=-1, keepdims=True)
        - normed * jnp.mean(scaled * normed, axis=-1, keepdims=True)
    )


def gelu_parts(pre):
    cumul = 0.5 * (1.0 + lax.erf(pre * ROOT_HALF))
    return (pre * cumul, cumul + pre * jnp.exp(-0.5 * pre * pre) * INV_ROOT_TAU)


def masked_scores(queries, keys, segs):
    scores = jnp.einsum(
        "qhd,khd->hqk", queries, keys, preferred_element_type=jnp.float32
    ) * HEAD_DIM ** (-0.5)
    allowed = segs[:, None] == segs[None, :]
    return jnp.where(allowed[None], scores, MASKED)


def forward_seq(items):
    queries, keys, values, segs = items
    masked = masked_scores(queries, keys, segs)
    top = jnp.max(masked, axis=-1, keepdims=True)
    lse = top + jnp.log(jnp.sum(jnp.exp(masked - top), axis=-1, keepdims=True))
    probs = jnp.exp(masked - lse).astype(jnp.bfloat16)
    context = jnp.einsum("hqk,khd->qhd", probs, values, preferred_element_type=jnp.float32)
    return (context.astype(jnp.bfloat16), lse)


def backward_seq(items):
    queries, keys, values, segs, lse, d_context = items
    masked = masked_scores(queries, keys, segs)
    probs = jnp.exp(masked - lse)
    probs_half = probs.astype(jnp.bfloat16)
    d_values = jnp.einsum("hqk,qhd->khd", probs_half, d_context, preferred_element_type=jnp.float32)
    d_probs = jnp.einsum("qhd,khd->hqk", d_context, values, preferred_element_type=jnp.float32)
    d_scores = (
        probs * (d_probs - jnp.sum(probs * d_probs, axis=-1, keepdims=True)) * HEAD_DIM ** (-0.5)
    )
    d_scores = d_scores.astype(jnp.bfloat16)
    d_queries = jnp.einsum("hqk,khd->qhd", d_scores, keys, preferred_element_type=jnp.float32)
    d_keys = jnp.einsum("hqk,qhd->khd", d_scores, queries, preferred_element_type=jnp.float32)
    return (d_queries, d_keys, d_values)


def contract_rows(left, right):
    return lax.dot_general(
        left, right, (((0,), (0,)), ((), ())), preferred_element_type=jnp.float32
    )


def contract_cols(left, right):
    return lax.dot_general(
        left, right, (((1,), (1,)), ((), ())), preferred_element_type=jnp.float32
    )


def per_device(
    block_input,
    segment_ids,
    qkv_weight,
    qv_bias,
    out_weight,
    out_bias,
    norm1_gain,
    norm1_bias,
    up_weight,
    up_bias,
    down_weight,
    down_bias,
    norm2_gain,
    norm2_bias,
    cotangent,
):
    width = qkv_weight.shape[2]
    seq_count, seq_len = segment_ids.shape
    heads_here = width // HEAD_DIM
    gathered = lax.all_gather(block_input, "tensor", axis=0, tiled=True)
    tokens = gathered.shape[0]
    projected = jnp.einsum("td,cdw->ctw", gathered, qkv_weight, preferred_element_type=jnp.float32)
    queries = (projected[0] + qv_bias[0]).astype(jnp.bfloat16)
    keys = projected[1].astype(jnp.bfloat16)
    values = (projected[2] + qv_bias[1]).astype(jnp.bfloat16)

    def per_sequence(arr):
        return arr.reshape(seq_count, seq_len, heads_here, HEAD_DIM)

    seq_queries = per_sequence(queries)
    seq_keys = per_sequence(keys)
    seq_values = per_sequence(values)
    context, lse = lax.map(forward_seq, (seq_queries, seq_keys, seq_values, segment_ids))
    context = context.reshape(tokens, width)
    piece = context
    attended = lax.psum_scatter(
        jnp.dot(piece, out_weight, preferred_element_type=jnp.float32).astype(jnp.bfloat16),
        "tensor",
        scatter_dimension=0,
        tiled=True,
    ).astype(jnp.float32)
    first = block_input.astype(jnp.float32) + attended + out_bias
    hidden, normed_one, inverse_one = layer_norm(first, norm1_gain, norm1_bias)
    hidden_half = lax.all_gather(hidden.astype(jnp.bfloat16), "tensor", axis=0, tiled=True)
    pre = jnp.dot(hidden_half, up_weight, preferred_element_type=jnp.float32) + up_bias
    act, slope = gelu_parts(pre)
    act_half = act.astype(jnp.bfloat16)
    piece = act_half
    down_sum = lax.psum_scatter(
        jnp.dot(piece, down_weight, preferred_element_type=jnp.float32).astype(jnp.bfloat16),
        "tensor",
        scatter_dimension=0,
        tiled=True,
    ).astype(jnp.float32)
    second = hidden + down_sum + down_bias
    output, normed_two, inverse_two = layer_norm(second, norm2_gain, norm2_bias)
    grad = cotangent.astype(jnp.float32)
    g_gain_two = jnp.sum(grad * normed_two, axis=0)
    g_bias_two = jnp.sum(grad, axis=0)
    d_second = norm_back(grad, normed_two, inverse_two, norm2_gain)
    g_down_bias = jnp.sum(d_second, axis=0)
    d_second_all = lax.all_gather(d_second.astype(jnp.bfloat16), "tensor", axis=0, tiled=True)
    g_down = contract_rows(act_half, d_second_all)
    d_pre = contract_cols(d_second_all, down_weight) * slope
    g_up_bias = jnp.sum(d_pre, axis=0)
    d_pre_half = d_pre.astype(jnp.bfloat16)
    g_up = contract_rows(hidden_half, d_pre_half)
    piece = d_pre_half
    d_hidden = d_second + lax.psum_scatter(
        contract_cols(piece, up_weight), "tensor", scatter_dimension=0, tiled=True
    )
    g_gain_one = jnp.sum(d_hidden * normed_one, axis=0)
    g_bias_one = jnp.sum(d_hidden, axis=0)
    d_first = norm_back(d_hidden, normed_one, inverse_one, norm1_gain)
    g_out_bias = jnp.sum(d_first, axis=0)
    d_first_all = lax.all_gather(d_first.astype(jnp.bfloat16), "tensor", axis=0, tiled=True)
    g_out = contract_rows(context, d_first_all)
    d_context = contract_cols(d_first_all, out_weight).astype(jnp.bfloat16)
    d_queries, d_keys, d_values = lax.map(
        backward_seq, (seq_queries, seq_keys, seq_values, segment_ids, lse, per_sequence(d_context))
    )
    d_queries = d_queries.reshape(tokens, width)
    d_keys = d_keys.reshape(tokens, width)
    d_values = d_values.reshape(tokens, width)
    g_qv_bias = jnp.stack([jnp.sum(d_queries, axis=0), jnp.sum(d_values, axis=0)])
    d_qkv = jnp.stack([d_queries, d_keys, d_values]).astype(jnp.bfloat16)
    g_qkv = jnp.einsum("td,ctw->cdw", gathered, d_qkv, preferred_element_type=jnp.float32)
    piece = d_qkv
    input_grad = (
        d_first
        + lax.psum_scatter(
            jnp.einsum("ctw,cdw->td", piece, qkv_weight, preferred_element_type=jnp.float32).astype(
                jnp.bfloat16
            ),
            "tensor",
            scatter_dimension=0,
            tiled=True,
        ).astype(jnp.float32)
    ).astype(jnp.bfloat16)
    g_qkv, g_qv_bias, g_out, g_up, g_up_bias, g_down = (
        lax.psum(g_qkv.astype(jnp.bfloat16), "dp").astype(jnp.float32),
        lax.psum(g_qv_bias.astype(jnp.bfloat16), "dp").astype(jnp.float32),
        lax.psum(g_out.astype(jnp.bfloat16), "dp").astype(jnp.float32),
        lax.psum(g_up.astype(jnp.bfloat16), "dp").astype(jnp.float32),
        lax.psum(g_up_bias.astype(jnp.bfloat16), "dp").astype(jnp.float32),
        lax.psum(g_down.astype(jnp.bfloat16), "dp").astype(jnp.float32),
    )
    g_out_bias, g_gain_one, g_bias_one, g_down_bias, g_gain_two, g_bias_two = lax.psum(
        (g_out_bias, g_gain_one, g_bias_one, g_down_bias, g_gain_two, g_bias_two), ("dp", "tensor")
    )
    return (
        output.astype(jnp.bfloat16),
        input_grad,
        g_qkv,
        g_qv_bias,
        g_out,
        g_out_bias,
        g_gain_one,
        g_bias_one,
        g_up,
        g_up_bias,
        g_down,
        g_down_bias,
        g_gain_two,
        g_bias_two,
    )


def solution(mesh):
    placed = (
        P(("dp", "tensor"), None),
        P("dp", None),
        P(None, None, "tensor"),
        P(None, "tensor"),
        P("tensor", None),
        P(),
        P(),
        P(),
        P(None, "tensor"),
        P("tensor"),
        P("tensor", None),
        P(),
        P(),
        P(),
        P(("dp", "tensor"), None),
    )
    return jax.shard_map(
        per_device,
        mesh=mesh,
        in_specs=placed,
        out_specs=(
            P(("dp", "tensor"), None),
            P(("dp", "tensor"), None),
            P(None, None, "tensor"),
            P(None, "tensor"),
            P("tensor", None),
            P(),
            P(),
            P(),
            P(None, "tensor"),
            P("tensor"),
            P("tensor", None),
            P(),
            P(),
            P(),
        ),
        check_vma=False,
    )
```

profile of v0, /device:TPU:0, one launch (start us, length us, event | category | flops | bytes accessed | tf_op | source)
XLA Modules:
  0.0 736.1 jit_solution(5672415623791416606)
XLA Ops:
  8.8 60.4 %all-gather.5.cloned.1.call-done = bf16[2048,1024]{1,0:T(8,128)(2,1)} async-done(((bf16[128,1024]{1,0:T(8,128)(2,1)}), bf16[2048,1024]{1,0:T(8,128)(2,1)}) %all-gather.5.cloned.1.call-update) | async-done | bytes 4194320 | tf_op jit(solution)/shard_map/all_gather | solution.py:102
  69.2 3.8 fusion.50
  74.6 6.2 while.26
  81.3 3.2 convolution_convert_fusion.1
  84.6 79.4 %reduce-scatter.5.cloned.1.call-done = bf16[128,1024]{1,0:T(8,128)(2,1)} async-done(((bf16[2048,1024]{1,0:T(8,128)(2,1)}), bf16[128,1024]{1,0:T(8,128)(2,1)}) %reduce-scatter.5.cloned.1.call-update) | async-done | bytes 262160 | tf_op jit(solution)/shard_map/reduce_scatter | solution.py:118
  168.2 54.9 %all-gather.7.cloned.1.call-done = bf16[2048,1024]{1,0:T(8,128)(2,1)} async-done(((bf16[128,1024]{1,0:T(8,128)(2,1)}), bf16[2048,1024]{1,0:T(8,128)(2,1)}) %all-gather.7.cloned.1.call-update) | async-done | bytes 4194320 | tf_op jit(solution)/shard_map/all_gather | solution.py:126
  223.1 4.9 multiply_convert_fusion.1
  227.9 3.2 convolution_convert_fusion
  231.3 79.4 %reduce-scatter.7.cloned.1.call-done = bf16[128,1024]{1,0:T(8,128)(2,1)} async-done(((bf16[2048,1024]{1,0:T(8,128)(2,1)}), bf16[128,1024]{1,0:T(8,128)(2,1)}) %reduce-scatter.7.cloned.1.call-update) | async-done | bytes 262160 | tf_op jit(solution)/shard_map/reduce_scatter | solution.py:131
  313.0 2.5 fusion.77
  316.5 54.7 %all-gather.9.cloned.1.call-done = bf16[2048,1024]{1,0:T(8,128)(2,1)} async-done(((bf16[128,1024]{1,0:T(8,128)(2,1)}), bf16[2048,1024]{1,0:T(8,128)(2,1)}) %all-gather.9.cloned.1.call-update) | async-done | bytes 4194320 | tf_op jit(solution)/shard_map/all_gather | solution.py:144
  371.2 5.3 fusion.84
  377.5 4.5 fusion.73
  382.1 101.2 %reduce-scatter.9.cloned.1.call-done = f32[128,1024]{1,0:T(8,128)} async-done(((f32[2048,1024]{1,0:T(8,128)}), f32[128,1024]{1,0:T(8,128)}) %reduce-scatter.9.cloned.1.call-update) | async-done | bytes 524304 | tf_op jit(solution)/shard_map/reduce_scatter | solution.py:151
  487.7 4.4 convolution_convert_fusion.3
  492.1 3.4 convolution_convert_fusion.4
  495.5 47.0 %all-gather.11.cloned.1.call-done = bf16[2048,1024]{1,0:T(8,128)(2,1)} async-done(((bf16[128,1024]{1,0:T(8,128)(2,1)}), bf16[2048,1024]{1,0:T(8,128)(2,1)}) %all-gather.11.cloned.1.call-update) | async-done | bytes 4194320 | tf_op jit(solution)/shard_map/all_gather | solution.py:158
  542.5 3.6 convolution_convert_fusion.2
  546.3 10.9 %while.27 = (s32[]{:T(128)}, f32[2,1024,1,64]{1,3,2,0:T(8,128)S(1)}, bf16[2,1024,1,64]{1,3,2,0:T(8,128)(2,1)S(1)}, f32[2,1024,1,64]{1,3,2,0:T(8,128)S(1)}, bf16[...) while((s32[]{:T(128)}, ...), condition=%wide.region_17.18_spmd, body=%wide.region_15.17_spmd.sunk | while | flops 682621952 | bytes 33203324 | solution.py:161
  558.9 3.8 convolution_convert_fusion.5
  564.8 3.2 bitcast_convert_fusion
  568.8 66.9 %all-reduce = (f32[1024]{0:T(1024)}, f32[1024]{0:T(1024)}, f32[1024]{0:T(1024)}, f32[1024]{0:T(1024)}, f32[1024]{0:T(1024)}, /*index=5*/f32[1024]{0:T(1024)}) all-reduce(f32[1024]{0:T(1024)S(1)} %copy-done.25, f32[1024]{0:T(1024)S(1)} %copy-done.23, f32[1024]{0:T(1024)S(1)} %copy-done.24, ...), channel_id=1, replica_groups=mesh['dp'=8,'tensor'=16] {'dp','tensor'}, use_global_device_ids=true, to_apply=%region_25.26 | all-reduce | flops 6144 | bytes 49152 | tf_op jit(solution)/shard_map/psum | solution.py:190
  635.7 17.7 %all-reduce.1 = (bf16[2,64]{1,0:T(2,128)(2,1)S(1)}, bf16[256]{0:T(256)(128)(2,1)S(1)}) all-reduce(bf16[2,64]{1,0:T(2,128)(2,1)S(1)} %pad_maximum_fusion, bf16[256]{0:T(256)(128)(2,1)S(1)} %copy-done.35), channel_id=1, replica_groups=mesh['dp'=8,'tensor'=16] {'dp'}, use_global_device_ids=true, to_apply=%region_22.23 | all-reduce | flops 384 | bytes 1536 | tf_op jit(solution)/shard_map/psum | solution.py:184
  662.5 65.4 %reduce-scatter.11.cloned.1.call-done = bf16[128,1024]{1,0:T(8,128)(2,1)} async-done(((bf16[2048,1024]{1,0:T(8,128)(2,1)}), bf16[128,1024]{1,0:T(8,128)(2,1)}) %reduce-scatter.11.cloned.1.call-update) | async-done | bytes 262160 | tf_op jit(solution)/shard_map/reduce_scatter | solution.py:173
  (174 shorter events, 48.7 us)
Async XLA Ops:
  7.2 215.9 %copy-start = (bf16[1024,256]{1,0:T(8,128)(2,1)S(1)}, bf16[1024,256]{1,0:T(8,128)(2,1)}, u32[]{:S(2)}) copy-start(bf16[1024,256]{1,0:T(8,128)(2,1)} %param.27) | copy-start | bytes 1572868
  7.2 62.0 %all-gather.5.cloned.1.call-start = ((), (), s32[]{:S(2)}) async-start(), calls=%async_computation.4 | async-start | bytes 4456448 | tf_op jit(solution)/shard_map/all_gather | solution.py:102
  7.9 156.0 %reduce-scatter.5.cloned.1.call-start = ((), (), s32[]{:S(2)}) async-start(), calls=%async_computation.5 | async-start | bytes 4456448 | tf_op jit(solution)/shard_map/reduce_scatter | solution.py:118
  81.2 82.7 %copy-start.2 = (bf16[128,1024]{1,0:T(8,128)(2,1)S(1)}, bf16[128,1024]{1,0:T(8,128)(2,1)}, u32[]{:S(2)}) copy-start(bf16[128,1024]{1,0:T(8,128)(2,1)} %param.19) | copy-start | bytes 786436
  81.2 82.7 %copy-start.13 = (f32[1024]{0:T(1024)S(1)}, f32[1024]{0:T(1024)}, u32[]{:S(2)}) copy-start(f32[1024]{0:T(1024)} %param.24) | copy-start | bytes 12292
  81.2 85.0 %copy-start.14 = (f32[1024]{0:T(1024)S(1)}, f32[1024]{0:T(1024)}, u32[]{:S(2)}) copy-start(f32[1024]{0:T(1024)} %param.25) | copy-start | bytes 12292
  81.2 85.0 %copy-start.17 = (f32[1024]{0:T(1024)S(1)}, f32[1024]{0:T(1024)}, u32[]{:S(2)}) copy-start(f32[1024]{0:T(1024)} %param.26) | copy-start | bytes 12292
  84.5 138.6 %copy-start.34 = (f32[256]{0:T(256)S(1)}, f32[256]{0:T(256)}, u32[]{:S(2)}) copy-start(f32[256]{0:T(256)} %param.28) | copy-start | bytes 3076
  84.5 138.5 %all-gather.7.cloned.1.call-start = ((), (), s32[]{:S(2)}) async-start(), calls=%async_computation.6 | async-start | bytes 4456448 | tf_op jit(solution)/shard_map/all_gather | solution.py:126
  168.1 142.5 %reduce-scatter.7.cloned.1.call-start = ((), (), s32[]{:S(2)}) async-start(), calls=%async_computation.7 | async-start | bytes 4456448 | tf_op jit(solution)/shard_map/reduce_scatter | solution.py:131
  231.1 79.6 %copy-start.3 = (bf16[128,1024]{1,0:T(8,128)(2,1)S(1)}, bf16[128,1024]{1,0:T(8,128)(2,1)}, u32[]{:S(2)}) copy-start(bf16[128,1024]{1,0:T(8,128)(2,1)} %reduce-scatter.5.cloned.1.call-done) | copy-start | bytes 786436
  231.1 79.6 %copy-start.18 = (f32[1024]{0:T(1024)S(1)}, f32[1024]{0:T(1024)}, u32[]{:S(2)}) copy-start(f32[1024]{0:T(1024)} %param.26) | copy-start | bytes 12292
  231.1 79.6 %copy-start.27 = (f32[128]{0:T(128)S(1)}, f32[128]{0:T(128)}, u32[]{:S(2)}) copy-start(f32[128]{0:T(128)} %copy-done.26) | copy-start | bytes 1540
  231.1 79.6 %copy-start.29 = (f32[128]{0:T(128)S(1)}, f32[128]{0:T(128)}, u32[]{:S(2)}) copy-start(f32[128]{0:T(128)} %copy-done.28) | copy-start | bytes 1540
  231.1 79.6 %copy-start.30 = (f32[1024]{0:T(1024)S(1)}, f32[1024]{0:T(1024)}, u32[]{:S(2)}) copy-start(f32[1024]{0:T(1024)} %param.30) | copy-start | bytes 12292
  231.2 81.1 %copy-start.7 = (bf16[128,1024]{1,0:T(8,128)(2,1)S(1)}, bf16[128,1024]{1,0:T(8,128)(2,1)}, u32[]{:S(2)}) copy-start(bf16[128,1024]{1,0:T(8,128)(2,1)} %param.33) | copy-start | bytes 786436
  231.2 81.1 %copy-start.19 = (f32[1024]{0:T(1024)S(1)}, f32[1024]{0:T(1024)}, u32[]{:S(2)}) copy-start(f32[1024]{0:T(1024)} %param.31) | copy-start | bytes 12292
  231.2 140.0 %all-gather.9.cloned.1.call-start = ((), (), s32[]{:S(2)}) async-start(), calls=%async_computation.8 | async-start | bytes 4456448 | tf_op jit(solution)/shard_map/all_gather | solution.py:144
  316.3 167.0 %reduce-scatter.9.cloned.1.call-start = ((), (), s32[]{:S(2)}) async-start(), calls=%async_computation.9 | async-start | bytes 8912896 | tf_op jit(solution)/shard_map/reduce_scatter | solution.py:151
  382.1 160.4 %all-gather.11.cloned.1.call-start = ((), (), s32[]{:S(2)}) async-start(), calls=%async_computation.10 | async-start | bytes 4456448 | tf_op jit(solution)/shard_map/all_gather | solution.py:158
  487.6 166.9 %all-reduce.5.cloned.1.call-start = ((), (), s32[]{:S(2)}) async-start(), calls=%async_computation.12 | async-start | bytes 3145728 | tf_op jit(solution)/shard_map/psum | solution.py:183
  564.5 163.3 %reduce-scatter.11.cloned.1.call-start = ((), (), s32[]{:S(2)}) async-start(), calls=%async_computation.11 | async-start | bytes 4456448 | tf_op jit(solution)/shard_map/reduce_scatter | solution.py:173
  568.1 67.6 %copy-start.35 = (bf16[256]{0:T(256)(128)(2,1)S(1)}, bf16[256]{0:T(256)(128)(2,1)}, u32[]{:S(2)}) copy-start(bf16[256]{0:T(256)(128)(2,1)} %get-tuple-element.221) | copy-start | bytes 1540
  568.1 161.5 %copy-start.1 = (bf16[1024,256]{1,0:T(8,128)(2,1)S(1)}, bf16[1024,256]{1,0:T(8,128)(2,1)}, u32[]{:S(2)}) copy-start(bf16[1024,256]{1,0:T(8,128)(2,1)} %param.27) | copy-start | bytes 1572868
  (21 other events, 249.8 us)
Sparse Core Ops, SparseCore 0:
  10.4 58.6 all-gather.4
  84.6 79.2 reduce-scatter.4
  168.3 54.7 all-gather.6
  231.3 79.3 reduce-scatter.6
  316.4 54.7 all-gather.8
  382.2 101.0 reduce-scatter.8
  487.7 54.7 all-gather.10
  564.6 78.7 all-reduce.4
  647.5 80.2 reduce-scatter.10
where the time goes:
time: 737 us; the launch traced here: 736 us
  waiting for transfers between devices  543 us (74%)
  blocking collectives  84.6 us (11%)
  matrix products  57.6 us (8%)
  other arithmetic  29.5 us (4%)
  between operations  14.4 us (2%)
    reduce_scatter x1, waiting for transfers between devices, per_device(): lax.psum_scatter(contract_cols(piece, up_weight), 'tensor', scatter_dimen...  101 us
    reduce_scatter x1, waiting for transfers between devices, per_device(): lax.psum_scatter(jnp.dot(piece, down_weight, preferred_element_type=jnp.f...  79.4 us
    reduce_scatter x1, waiting for transfers between devices, per_device(): lax.psum_scatter(jnp.dot(piece, out_weight, preferred_element_type=jnp.fl...  79.4 us
    psum x1, blocking collectives, per_device(): lax.psum((g_out_bias, g_gain_one, g_bias_one, g_down_bias, g_gain_two, g_...  66.9 us
    reduce_scatter x1, waiting for transfers between devices, per_device(): lax.psum_scatter(jnp.einsum('ctw,cdw->td', piece, qkv_weight, preferred_e...  65.4 us
    all_gather x1, waiting for transfers between devices, per_device(): gathered = lax.all_gather(block_input, 'tensor', axis=0, tiled=True)  60.4 us
    all_gather x1, waiting for transfers between devices, per_device(): lax.all_gather(hidden.astype(jnp.bfloat16), 'tensor', axis=0, tiled=True)  54.9 us
    all_gather x1, waiting for transfers between devices, per_device(): lax.all_gather(d_second.astype(jnp.bfloat16), 'tensor', axis=0, tiled=True)  54.7 us
  transfers between devices with their start and end apart: 9, of which 8 were waited for; matrix products, arithmetic and copies ran while one was open for 3% of the time, Pallas kernels for 0%

commit v1 on v0

--- a/solution.py
+++ b/solution.py
@@ -1,6 +1,8 @@
 import jax
 import jax.numpy as jnp
 from jax import lax
+from jax.experimental import pallas as pl
+from jax.experimental.pallas import tpu as pltpu
 from jax.sharding import PartitionSpec as P
 
 HEAD_DIM = 64
@@ -77,6 +79,240 @@
     return lax.dot_general(
         left, right, (((1,), (1,)), ((), ())), preferred_element_type=jnp.float32
     )
+
+
+MESH = pl.DeviceIdType.MESH
+
+
+def places():
+    dp, me = lax.axis_index("dp"), lax.axis_index("tensor")
+    core, x, z = lax.rem(me, 2), lax.rem(me // 2, 4), me // 8
+    right, left = lax.rem(x + 1, 4), lax.rem(x + 3, 4)
+
+    def at(z_at, x_at, core_at):
+        return z_at * 8 + x_at * 2 + core_at
+
+    return dp, me, core, x, z, right, left, at
+
+
+def meet(dp, partners):
+    barrier = pltpu.get_barrier_semaphore()
+    for partner in partners:
+        pl.semaphore_signal(barrier, inc=1, device_id=(dp, partner), device_id_type=MESH)
+    pl.semaphore_wait(barrier, len(partners))
+
+
+def gather_kernel(x_ref, out_ref, send, recv, local):
+    dp, me, core, x, z, right, left, at = places()
+    far, other = 1 - z, 1 - core
+    across = lax.rem(x + 2, 4)
+    z_peer, c_peer = at(far, x, core), at(z, x, other)
+    r_peer, l_peer = at(z, right, core), at(z, left, core)
+    meet(dp, (z_peer, c_peer, r_peer, l_peer))
+    started = []
+    numbers = {}
+
+    def copy(name, src, slot, half, peer):
+        number = numbers.setdefault(name, len(numbers))
+        return pltpu.make_async_remote_copy(
+            src_ref=src,
+            dst_ref=out_ref.at[slot, half],
+            send_sem=send.at[number],
+            recv_sem=recv.at[number],
+            device_id=(dp, peer),
+            device_id_type=MESH,
+        )
+
+    def push(name, src, slot, half, peer):
+        moving = copy(name, src, slot, half, peer)
+        moving.start()
+        started.append(moving)
+
+    def arrived(name, slot, half):
+        copy(name, out_ref.at[slot, half], slot, half, me).wait_recv()
+
+    def share(level, name_x, slot, half):
+        push(("c", level, name_x, half), out_ref.at[slot, half], slot, half, c_peer)
+
+    for half in range(2):
+        push(("z", half), x_ref.at[half], me, half, z_peer)
+    for step in range(2):
+        push(("r", 0, step), x_ref.at[step], me, step, r_peer)
+        push(("l", 0, 1 - step), x_ref.at[1 - step], me, 1 - step, l_peer)
+    for half in range(2):
+        push(("c", 0, "own", half), x_ref.at[half], me, half, c_peer)
+    keep = pltpu.make_async_copy(x_ref, out_ref.at[me], local)
+    keep.start()
+
+    for level, z_at in ((0, z), (1, far)):
+        if level == 1:
+            own = at(far, x, core)
+            for half in range(2):
+                arrived(("z", half), own, half)
+                push(("r", 1, half), out_ref.at[own, half], own, half, r_peer)
+                push(("l", 1, half), out_ref.at[own, half], own, half, l_peer)
+                share(1, "own", own, half)
+        from_left, from_right = at(z_at, left, core), at(z_at, right, core)
+        arrived(("r", level, 0), from_left, 0)
+        push(("rr", level), out_ref.at[from_left, 0], from_left, 0, r_peer)
+        share(level, "left", from_left, 0)
+        arrived(("l", level, 1), from_right, 1)
+        push(("ll", level), out_ref.at[from_right, 1], from_right, 1, l_peer)
+        share(level, "right", from_right, 1)
+        arrived(("r", level, 1), from_left, 1)
+        share(level, "left", from_left, 1)
+        arrived(("l", level, 0), from_right, 0)
+        share(level, "right", from_right, 0)
+    for level, z_at in ((0, z), (1, far)):
+        beyond = at(z_at, across, core)
+        arrived(("rr", level), beyond, 0)
+        share(level, "across", beyond, 0)
+        arrived(("ll", level), beyond, 1)
+        share(level, "across", beyond, 1)
+    for level, z_at in ((0, z), (1, far)):
+        for name_x, x_at in (("own", x), ("left", left), ("right", right), ("across", across)):
+            for half in range(2):
+                arrived(("c", level, name_x, half), at(z_at, x_at, other), half)
+    keep.wait()
+    for moving in started:
+        moving.wait_send()
+
+
+def gather_tensor(block):
+    rows, width = block.shape
+    half = rows // 2
+    out = pl.pallas_call(
+        gather_kernel,
+        out_shape=jax.ShapeDtypeStruct((16, 2, half, width), block.dtype),
+        in_specs=[pl.BlockSpec(memory_space=pltpu.VMEM)],
+        out_specs=pl.BlockSpec(memory_space=pltpu.VMEM),
+        scratch_shapes=[
+            pltpu.SemaphoreType.DMA((30,)),
+            pltpu.SemaphoreType.DMA((30,)),
+            pltpu.SemaphoreType.DMA,
+        ],
+        compiler_params=pltpu.CompilerParams(
+            collective_id=0, has_side_effects=True, vmem_limit_bytes=32 << 20
+        ),
+        cost_estimate=pl.CostEstimate(flops=0, bytes_accessed=60 << 20, transcendentals=0),
+    )(block.reshape(2, half, width))
+    return out.reshape(16 * rows, width)
+
+
+def scatter_kernel(p_ref, out_ref, from_core, ring, from_z, send, recv):
+    dp, me, core, x, z, right, left, at = places()
+    far, other = 1 - z, 1 - core
+    across = lax.rem(x + 2, 4)
+    z_peer, c_peer = at(far, x, core), at(z, x, other)
+    r_peer, l_peer = at(z, right, core), at(z, left, core)
+    meet(dp, (z_peer, c_peer, r_peer, l_peer))
+    started = []
+    numbers = {}
+    rows = out_ref.shape[1]
+
+    def copy(name, src, dst, peer):
+        number = numbers.setdefault(name, len(numbers))
+        return pltpu.make_async_remote_copy(
+            src_ref=src,
+            dst_ref=dst,
+            send_sem=send.at[number],
+            recv_sem=recv.at[number],
+            device_id=(dp, peer),
+            device_id_type=MESH,
+        )
+
+    def push(name, src, dst, peer):
+        moving = copy(name, src, dst, peer)
+        moving.start()
+        started.append(moving)
+
+    def arrived(name, dst):
+        copy(name, dst, dst, me).wait_recv()
+
+    def total(dst, *terms):
+        @pl.loop(0, rows // 16)
+        def _(step):
+            here = pl.ds(pl.multiple_of(step * 16, 16), 16)
+            value = terms[0][here, :].astype(jnp.float32)
+            for term in terms[1:]:
+                value = value + term[here, :].astype(jnp.float32)
+            dst[here, :] = value.astype(dst.dtype)
+
+    order = [(level, kind) for level in (0, 1) for kind in range(4)]
+    z_of = (far, z)
+    x_of = (across, right, left, x)
+    for level, kind in order:
+        slot = level * 4 + kind
+        push(
+            ("c", slot),
+            p_ref.at[at(z_of[level], x_of[kind], other)],
+            from_core.at[slot],
+            c_peer,
+        )
+    for level in range(2):
+        base = level * 6
+
+        def mine(kind, half):
+            return from_core.at[level * 4 + kind, half]
+
+        for kind in range(4):
+            slot = level * 4 + kind
+            arrived(("c", slot), from_core.at[slot])
+            block = at(z_of[level], x_of[kind], core)
+            for half in range(2):
+                total(mine(kind, half), p_ref.at[block, half], mine(kind, half))
+            if kind == 0:
+                push(("ar", level), mine(0, 0), ring.at[base], r_peer)
+                push(("al", level), mine(0, 1), ring.at[base + 1], l_peer)
+            if kind == 1:
+                push(("b", level, 2), mine(1, 1), ring.at[base + 2], r_peer)
+            if kind == 2:
+                push(("b", level, 3), mine(2, 0), ring.at[base + 3], l_peer)
+        arrived(("ar", level), ring.at[base])
+        total(mine(1, 0), ring.at[base], mine(1, 0))
+        push(("b", level, 4), mine(1, 0), ring.at[base + 4], r_peer)
+        arrived(("al", level), ring.at[base + 1])
+        total(mine(2, 1), ring.at[base + 1], mine(2, 1))
+        push(("b", level, 5), mine(2, 1), ring.at[base + 5], l_peer)
+    for level in range(2):
+        base = level * 6
+        own = level * 4 + 3
+        for half, parts in ((1, (2, 5)), (0, (3, 4))):
+            for part in parts:
+                arrived(("b", level, part), ring.at[base + part])
+            terms = [from_core.at[own, half]] + [ring.at[base + part] for part in parts]
+            if level == 0:
+                total(from_core.at[own, half], *terms)
+                push(("z", half), from_core.at[own, half], from_z.at[half], z_peer)
+            else:
+                arrived(("z", half), from_z.at[half])
+                total(out_ref.at[half], *terms, from_z.at[half])
+    for moving in started:
+        moving.wait_send()
+
+
+def scatter_tensor(whole):
+    tokens, width = whole.shape
+    half = tokens // 32
+    wide = whole.dtype == jnp.float32
+    out = pl.pallas_call(
+        scatter_kernel,
+        out_shape=jax.ShapeDtypeStruct((2, half, width), jnp.float32),
+        in_specs=[pl.BlockSpec(memory_space=pltpu.VMEM)],
+        out_specs=pl.BlockSpec(memory_space=pltpu.VMEM),
+        scratch_shapes=[
+            pltpu.VMEM((8, 2, half, width), whole.dtype),
+            pltpu.VMEM((12, half, width), whole.dtype),
+            pltpu.VMEM((2, half, width), whole.dtype),
+            pltpu.SemaphoreType.DMA((22,)),
+            pltpu.SemaphoreType.DMA((22,)),
+        ],
+        compiler_params=pltpu.CompilerParams(
+            collective_id=2 if wide else 1, has_side_effects=True, vmem_limit_bytes=40 << 20
+        ),
+        cost_estimate=pl.CostEstimate(flops=0, bytes_accessed=80 << 20, transcendentals=0),
+    )(whole.reshape(16, 2, half, width))
+    return out.reshape(2 * half, width)
 
 
 def per_device(
@@ -99,7 +335,7 @@
     width = qkv_weight.shape[2]
     seq_count, seq_len = segment_ids.shape
     heads_here = width // HEAD_DIM
-    gathered = lax.all_gather(block_input, "tensor", axis=0, tiled=True)
+    gathered = gather_tensor(block_input)
     tokens = gathered.shape[0]
     projected = jnp.einsum("td,cdw->ctw", gathered, qkv_weight, preferred_element_type=jnp.float32)
     queries = (projected[0] + qv_bias[0]).astype(jnp.bfloat16)
@@ -115,25 +351,19 @@
     context, lse = lax.map(forward_seq, (seq_queries, seq_keys, seq_values, segment_ids))
     context = context.reshape(tokens, width)
     piece = context
-    attended = lax.psum_scatter(
-        jnp.dot(piece, out_weight, preferred_element_type=jnp.float32).astype(jnp.bfloat16),
-        "tensor",
-        scatter_dimension=0,
-        tiled=True,
-    ).astype(jnp.float32)
+    attended = scatter_tensor(
+        jnp.dot(piece, out_weight, preferred_element_type=jnp.float32).astype(jnp.bfloat16)
+    )
     first = block_input.astype(jnp.float32) + attended + out_bias
     hidden, normed_one, inverse_one = layer_norm(first, norm1_gain, norm1_bias)
-    hidden_half = lax.all_gather(hidden.astype(jnp.bfloat16), "tensor", axis=0, tiled=True)
+    hidden_half = gather_tensor(hidden.astype(jnp.bfloat16))
     pre = jnp.dot(hidden_half, up_weight, preferred_element_type=jnp.float32) + up_bias
     act, slope = gelu_parts(pre)
     act_half = act.astype(jnp.bfloat16)
     piece = act_half
-    down_sum = lax.psum_scatter(
-        jnp.dot(piece, down_weight, preferred_element_type=jnp.float32).astype(jnp.bfloat16),
-        "tensor",
-        scatter_dimension=0,
-        tiled=True,
-    ).astype(jnp.float32)
+    down_sum = scatter_tensor(
+        jnp.dot(piece, down_weight, preferred_element_type=jnp.float32).astype(jnp.bfloat16)
+    )
     second = hidden + down_sum + down_bias
     output, normed_two, inverse_two = layer_norm(second, norm2_gain, norm2_bias)
     grad = cotangent.astype(jnp.float32)
@@ -141,21 +371,19 @@
     g_bias_two = jnp.sum(grad, axis=0)
     d_second = norm_back(grad, normed_two, inverse_two, norm2_gain)
     g_down_bias = jnp.sum(d_second, axis=0)
-    d_second_all = lax.all_gather(d_second.astype(jnp.bfloat16), "tensor", axis=0, tiled=True)
+    d_second_all = gather_tensor(d_second.astype(jnp.bfloat16))
     g_down = contract_rows(act_half, d_second_all)
     d_pre = contract_cols(d_second_all, down_weight) * slope
     g_up_bias = jnp.sum(d_pre, axis=0)
     d_pre_half = d_pre.astype(jnp.bfloat16)
     g_up = contract_rows(hidden_half, d_pre_half)
     piece = d_pre_half
-    d_hidden = d_second + lax.psum_scatter(
-        contract_cols(piece, up_weight), "tensor", scatter_dimension=0, tiled=True
-    )
+    d_hidden = d_second + scatter_tensor(contract_cols(piece, up_weight))
     g_gain_one = jnp.sum(d_hidden * normed_one, axis=0)
     g_bias_one = jnp.sum(d_hidden, axis=0)
     d_first = norm_back(d_hidden, normed_one, inverse_one, norm1_gain)
     g_out_bias = jnp.sum(d_first, axis=0)
-    d_first_all = lax.all_gather(d_first.astype(jnp.bfloat16), "tensor", axis=0, tiled=True)
+    d_first_all = gather_tensor(d_first.astype(jnp.bfloat16))
     g_out = contract_rows(context, d_first_all)
     d_context = contract_cols(d_first_all, out_weight).astype(jnp.bfloat16)
     d_queries, d_keys, d_values = lax.map(
@@ -170,14 +398,11 @@
     piece = d_qkv
     input_grad = (
         d_first
-        + lax.psum_scatter(
+        + scatter_tensor(
             jnp.einsum("ctw,cdw->td", piece, qkv_weight, preferred_element_type=jnp.float32).astype(
                 jnp.bfloat16
-            ),
-            "tensor",
-            scatter_dimension=0,
-            tiled=True,
-        ).astype(jnp.float32)
+            )
+        )
     ).astype(jnp.bfloat16)
     g_qkv, g_qv_bias, g_out, g_up, g_up_bias, g_down = (
         lax.psum(g_qkv.astype(jnp.bfloat16), "dp").astype(jnp.float32),

time: 737 us -> 375 us (0.51)
  waiting for transfers between devices: 543 us -> 0.02 us
  Pallas kernels: 0 us -> 217 us
  matrix products: 57.6 us -> 33.3 us
  other arithmetic: 29.5 us -> 17.4 us
    reduce_scatter x4 -> x0, waiting for transfers between devices: 325 us -> none  [the longest x1 101 us: per_device(): lax.psum_scatter(contract_cols(piece, up_weight), 'tensor', scatter_dimen...]
    pallas_call x0 -> x8, Pallas kernels: none -> 217 us  [the longest x4 126 us: scatter_tensor(): pl.pallas_call(scatter_kernel, out_shape=jax.ShapeDtypeStruct((2, half, w...]
    all_gather x4 -> x0, waiting for transfers between devices: 217 us -> none  [the longest x1 60.4 us: per_device(): gathered = lax.all_gather(block_input, 'tensor', axis=0, tiled=True)]
    dot_general x3, matrix products: 13.4 us -> 4.55 us  [contract_cols(): lax.dot_general(left, right, (((1,), (1,)), ((), ())), preferred_element_...]
  transfers between devices with their start and end apart: 9 -> 1, of which waited for: 8 -> 0; matrix products, arithmetic and copies ran while one was open for 3% -> 1% of each run, Pallas kernels for 0% -> 7%
where the time goes in v1:
time: 375 us; the launch traced here: 374 us
  Pallas kernels  217 us (58%)
  blocking collectives  85 us (23%)
  matrix products  33.3 us (9%)
  other arithmetic  17.4 us (5%)
  between operations  14.7 us (4%)
  local copies, waits for them, and re-layouts  6.31 us (2%)
    pallas_call x4, Pallas kernels, scatter_tensor(): pl.pallas_call(scatter_kernel, out_shape=jax.ShapeDtypeStruct((2, half, w...  126 us
    pallas_call x4, Pallas kernels, gather_tensor(): pl.pallas_call(gather_kernel, out_shape=jax.ShapeDtypeStruct((16, 2, half...  91.5 us
    psum x1, blocking collectives, per_device(): lax.psum((g_out_bias, g_gain_one, g_bias_one, g_down_bias, g_gain_two, g_...  65.6 us
    psum x1, blocking collectives, per_device(): lax.psum(g_qv_bias.astype(jnp.bfloat16), 'dp').astype(jnp.float32)  19.4 us
  transfers between devices with their start and end apart: 1, of which 0 were waited for; matrix products, arithmetic and copies ran while one was open for 1% of the time, Pallas kernels for 7%

profile of v1, /device:TPU:0, one launch (start us, length us, event | category | flops | bytes accessed | tf_op | source)
XLA Modules:
  0.0 374.3 jit_solution(10815331749383542858)
XLA Ops:
  8.3 25.9 %shard_map.254 = bf16[16,2,64,1024]{3,2,1,0:T(8,128)(2,1)S(1)} custom-call(bf16[2,64,1024]{2,1,0:T(8,128)(2,1)S(1)} %bitcast.215), custom_call_target="tpu_custom_call" | custom-call | bytes 62914560 | tf_op jit(solution)/shard_map/pallas_call | solution.py:184
  34.2 1.9 copy-done.2
  36.1 1.5 convolution_bitcast_fusion.2
  39.3 6.2 %while.26 = (s32[]{:T(128)}, bf16[2,1024,1,64]{1,3,2,0:T(8,128)(2,1)S(1)}, f32[2,1,1024,1]{2,3,1,0:T(1,128)S(1)}, bf16[2,1024,1,64]{1,3,2,0:T(8,128)(2,1)S(1)}, ...) while((s32[]{:T(128)}, ...), condition=%wide.region_3.4_spmd, body=%wide.region_0.3_spmd.sunk | while | flops 283180032 | bytes 13174885 | solution.py:351
  47.2 25.5 %shard_map.255 = f32[2,64,1024]{2,1,0:T(8,128)S(1)} custom-call(bf16[16,2,64,1024]{3,2,1,0:T(8,128)(2,1)S(1)} %bitcast.207), custom_call_target="tpu_custom_call" | custom-call | bytes 83886080 | tf_op jit(solution)/shard_map/pallas_call | solution.py:298
  73.3 22.4 %shard_map.256 = bf16[16,2,64,1024]{3,2,1,0:T(8,128)(2,1)S(1)} custom-call(bf16[2,64,1024]{2,1,0:T(8,128)(2,1)S(1)} %bitcast.218), custom_call_target="tpu_custom_call" | custom-call | bytes 62914560 | tf_op jit(solution)/shard_map/pallas_call | solution.py:184
  98.4 27.7 %shard_map.257 = f32[2,64,1024]{2,1,0:T(8,128)S(1)} custom-call(bf16[16,2,64,1024]{3,2,1,0:T(8,128)(2,1)S(1)} %bitcast.206), custom_call_target="tpu_custom_call" | custom-call | bytes 83886080 | tf_op jit(solution)/shard_map/pallas_call | solution.py:298
  128.0 21.4 %shard_map.258 = bf16[16,2,64,1024]{3,2,1,0:T(8,128)(2,1)S(1)} custom-call(bf16[2,64,1024]{2,1,0:T(8,128)(2,1)S(1)} %bitcast.216), custom_call_target="tpu_custom_call" | custom-call | bytes 62914560 | tf_op jit(solution)/shard_map/pallas_call | solution.py:184
  149.4 2.1 convolution_convert_fusion.3
  151.5 1.9 fusion.77
  153.4 2.1 convolution_convert_fusion.4
  156.7 44.9 %shard_map.259 = f32[2,64,1024]{2,1,0:T(8,128)S(1)} custom-call(f32[16,2,64,1024]{3,2,1,0:T(8,128)S(1)} %bitcast.203), custom_call_target="tpu_custom_call" | custom-call | bytes 83886080 | tf_op jit(solution)/shard_map/pallas_call | solution.py:298
  202.2 21.8 %shard_map.260 = bf16[16,2,64,1024]{3,2,1,0:T(8,128)(2,1)S(1)} custom-call(bf16[2,64,1024]{2,1,0:T(8,128)(2,1)S(1)} %bitcast.217), custom_call_target="tpu_custom_call" | custom-call | bytes 62914560 | tf_op jit(solution)/shard_map/pallas_call | solution.py:184
  224.0 1.5 convolution_convert_fusion.6
  227.1 11.1 %while.27 = (s32[]{:T(128)}, f32[2,1024,1,64]{1,3,2,0:T(8,128)S(1)}, bf16[2,1024,1,64]{1,3,2,0:T(8,128)(2,1)S(1)}, f32[2,1024,1,64]{1,3,2,0:T(8,128)S(1)}, bf16[...) while((s32[]{:T(128)}, ...), condition=%wide.region_14.15_spmd, body=%wide.region_12.14_spmd.sunk | while | flops 682621952 | bytes 33203324 | solution.py:389
  233.6 1.5 multiply_reduce_fusion.7
  239.9 4.0 %fusion.50 = bf16[3,1024,64]{1,2,0:T(8,128)(2,1)} fusion(bf16[3,2048,64]{1,2,0:T(8,128)(2,1)S(1)} %constant_dynamic-update-slice_fusion.1, bf16[2048,1024,1]{1,0,2:T(8,128)(2,1)} %bitcast.210), kind=kOutput, calls=%fused_computation.72 | convolution fusion | flops 805502976 | bytes 5373952 | tf_op jit(solution)/shard_map/td,ctw->cdw/dot_general | solution.py:397
  243.9 19.4 %all-reduce.1 = (bf16[2,64]{1,0:T(2,128)(2,1)S(1)}, bf16[256]{0:T(256)(128)(2,1)S(1)}) all-reduce(bf16[2,64]{1,0:T(2,128)(2,1)S(1)} %pad_maximum_fusion, bf16[256]{0:T(256)(128)(2,1)S(1)} %get-tuple-element.223), channel_id=1, replica_groups=mesh['dp'=8,'tensor'=16] {'dp'}, use_global_device_ids=true, to_apply=%region_18.19 | all-reduce | flops 384 | bytes 1536 | tf_op jit(solution)/shard_map/psum | solution.py:409
  265.8 27.6 %shard_map.261 = f32[2,64,1024]{2,1,0:T(8,128)S(1)} custom-call(bf16[16,2,64,1024]{3,2,1,0:T(8,128)(2,1)S(1)} %bitcast.208), custom_call_target="tpu_custom_call" | custom-call | bytes 83886080 | tf_op jit(solution)/shard_map/pallas_call | solution.py:298
  293.4 65.6 %all-reduce = (f32[1024]{0:T(1024)}, f32[1024]{0:T(1024)}, f32[1024]{0:T(1024)}, f32[1024]{0:T(1024)}, f32[1024]{0:T(1024)}, /*index=5*/f32[1024]{0:T(1024)}) all-reduce(f32[1024]{0:T(1024)S(1)} %get-tuple-element.201, f32[1024]{0:T(1024)S(1)} %get-tuple-element.145, ...), channel_id=1, replica_groups=mesh['dp'=8,'tensor'=16] {'dp','tensor'}, use_global_device_ids=true, to_apply=%region_21.22 | all-reduce | flops 6144 | bytes 49152 | tf_op jit(solution)/shard_map/psum | solution.py:415
  359.7 1.6 convert_element_type.150
  361.3 2.0 convert_element_type.147
  363.3 2.1 convert_element_type.152
  365.4 2.1 convert_element_type.156
  (128 shorter events, 32.9 us)
Async XLA Ops:
  7.2 88.5 %copy-start = (bf16[1024,256]{1,0:T(8,128)(2,1)S(1)}, bf16[1024,256]{1,0:T(8,128)(2,1)}, u32[]{:S(2)}) copy-start(bf16[1024,256]{1,0:T(8,128)(2,1)} %param.27) | copy-start | bytes 1572868
  7.2 352.5 %all-reduce.5.cloned.1.call-start = ((), (), s32[]{:S(2)}) async-start(), calls=%async_computation | async-start | bytes 3145728 | tf_op jit(solution)/shard_map/psum | solution.py:408
  7.3 1.0 copy-start.3
  8.3 27.8 %copy-start.18 = (bf16[3,1024,64]{1,2,0:T(8,128)(2,1)S(1)}, bf16[3,1024,64]{1,2,0:T(8,128)(2,1)}, u32[]{:S(2)}) copy-start(bf16[3,1024,64]{1,2,0:T(8,128)(2,1)} %param.21) | copy-start | bytes 1179652
  34.2 1.9 copy-start.2
  36.1 1.7 copy-start.17
  37.7 1.6 copy-start.10
  39.3 6.6 %copy-start.7 = (bf16[64,1024]{1,0:T(8,128)(2,1)S(1)}, bf16[64,1024]{1,0:T(8,128)(2,1)}, u32[]{:S(2)}) copy-start(bf16[64,1024]{1,0:T(8,128)(2,1)} %param.23) | copy-start | bytes 393220
  45.9 26.8 %copy-start.4 = (bf16[128,1024]{1,0:T(8,128)(2,1)S(1)}, bf16[128,1024]{1,0:T(8,128)(2,1)}, u32[]{:S(2)}) copy-start(bf16[128,1024]{1,0:T(8,128)(2,1)} %param.19) | copy-start | bytes 786436
  45.9 26.8 %copy-start.14 = (f32[1024]{0:T(1024)S(1)}, f32[1024]{0:T(1024)}, u32[]{:S(2)}) copy-start(f32[1024]{0:T(1024)} %param.24) | copy-start | bytes 12292
  47.2 25.9 %copy-start.11 = (f32[1024]{0:T(1024)S(1)}, f32[1024]{0:T(1024)}, u32[]{:S(2)}) copy-start(f32[1024]{0:T(1024)} %param.25) | copy-start | bytes 12292
  47.2 25.9 %copy-start.12 = (f32[1024]{0:T(1024)S(1)}, f32[1024]{0:T(1024)}, u32[]{:S(2)}) copy-start(f32[1024]{0:T(1024)} %param.26) | copy-start | bytes 12292
  72.7 23.0 %copy-start.20 = (f32[256]{0:T(256)S(1)}, f32[256]{0:T(256)}, u32[]{:S(2)}) copy-start(f32[256]{0:T(256)} %param.28) | copy-start | bytes 3076
  95.7 1.4 copy-start.6
  98.4 27.8 %copy-start.15 = (f32[1024]{0:T(1024)S(1)}, f32[1024]{0:T(1024)}, u32[]{:S(2)}) copy-start(f32[1024]{0:T(1024)} %param.30) | copy-start | bytes 12292
  98.4 28.3 %copy-start.5 = (bf16[128,1024]{1,0:T(8,128)(2,1)S(1)}, bf16[128,1024]{1,0:T(8,128)(2,1)}, u32[]{:S(2)}) copy-start(bf16[128,1024]{1,0:T(8,128)(2,1)} %param.33) | copy-start | bytes 786436
  98.4 28.3 %copy-start.13 = (f32[1024]{0:T(1024)S(1)}, f32[1024]{0:T(1024)}, u32[]{:S(2)}) copy-start(f32[1024]{0:T(1024)} %param.31) | copy-start | bytes 12292
  98.4 28.6 %copy-start.16 = (f32[1024]{0:T(1024)S(1)}, f32[1024]{0:T(1024)}, u32[]{:S(2)}) copy-start(f32[1024]{0:T(1024)} %param.32) | copy-start | bytes 12292
  225.5 1.6 copy-start.8
  225.5 1.7 copy-start.9
  239.9 24.6 %copy-start.19 = (bf16[3,1024,64]{1,2,0:T(8,128)(2,1)S(1)}, bf16[3,1024,64]{1,2,0:T(8,128)(2,1)}, u32[]{:S(2)}) copy-start(bf16[3,1024,64]{1,2,0:T(8,128)(2,1)} %param.21) | copy-start | bytes 1179652
  265.8 101.7 %copy-start.1 = (bf16[1024,256]{1,0:T(8,128)(2,1)S(1)}, bf16[1024,256]{1,0:T(8,128)(2,1)}, u32[]{:S(2)}) copy-start(bf16[1024,256]{1,0:T(8,128)(2,1)} %param.27) | copy-start | bytes 1572868
Sparse Core Ops, SparseCore 0:
  244.0 80.7 all-reduce.4
